TPU v7x, 32 devices: a whole 2x2x4 slice. The times are simulated.
32 devices in a mesh: expert: 16 (over z, y, x), dp: 2 (over core).
Axes of the slice: x: 2, y: 2, z: 4, core: 2. Of those that a mesh axis runs over, the one named last changes fastest.
Arguments:
- pooled: bfloat16 [8192, 256], P(('expert', 'dp')), may hold values from -6 to 6
- routes: int32 [8192, 2], P(('expert', 'dp')), may hold values from 0 to 15, all different within a row; in each aligned block of 256 rows (0 to 255, 256 to 511, ...) at most 48 rows name the same one
- labels: int32 [8192, 2], P(('expert', 'dp')), may hold values from 0 to 1
- in_weight: bfloat16 [16, 4096, 256], P('expert'), may hold values from -0.375 to 0.375
- out_weight: bfloat16 [16, 4096, 256], P('expert'), may hold values from -0.09375 to 0.09375
- gate_weight: bfloat16 [16, 2, 256], replicated, may hold values from -0.375 to 0.375
- tower_weight: float32 [2, 256], replicated, may hold values from -0.375 to 0.375
- tower_bias: float32 [2], replicated, may hold values from -3 to 3
- bag_rows: int32 [16384], P(('expert', 'dp')), may hold values from 0 to 1023
- bag_sample: int32 [16384], P(('expert', 'dp')), may hold values from 0 to 255
- bag_weight: float32 [16384], P(('expert', 'dp')), may hold values from 0.5 to 2
- row_table: float32 [16384, 256], P('expert'), may hold values from -6 to 6
Outputs:
- in_grad: float32 [16, 4096, 256], P('expert', 'dp')
- out_grad: float32 [16, 4096, 256], P('expert', 'dp')
- gate_grad: float32 [16, 2, 256], P('expert')
- tower_grad: float32 [2, 256], replicated
- new_table: float32 [16384, 256], P('expert')
Inputs may be any that keep to these rules, and one draw needn't show every extreme that they name: `routes`: within each device's 256 rows no expert is named more than 48 times, a bound that some block reaches; a row's two experts differ.
All inputs are finite; a program needn't handle non-finite values.
Results may differ from a plain program's by a relative error of at most 0.0041.
Values may be sent and summed in bfloat16 or wider, within the bound.
A program may use at most 128 MiB of HBM per device.

v0:
```python
import jax
import jax.numpy as jnp
from jax import lax
from jax.sharding import PartitionSpec as P

LOSS_SCALE = 32.0
STEP_SIZE = 0.25
HIGH = lax.Precision.HIGHEST


def silu_grad(pre_silu):
    sigma = jax.nn.sigmoid(pre_silu)
    return sigma * (1.0 + pre_silu * (1.0 - sigma))


def route_slots(routes, owner_count, capacity):
    flat_routes = routes.reshape(-1)
    matches = flat_routes[:, None] == jnp.arange(owner_count, dtype=jnp.int32)[None, :]
    ranks = jnp.cumsum(matches.astype(jnp.int32), axis=0) - 1
    slot_of = jnp.sum(jnp.where(matches, ranks, 0), axis=1)
    return flat_routes * capacity + slot_of


def contract_first(left, right):
    return lax.dot_general(
        left, right, (((0,), (0,)), ((), ())), preferred_element_type=jnp.float32
    )


def contract_last(left, right):
    return lax.dot_general(
        left, right, (((1,), (1,)), ((), ())), preferred_element_type=jnp.float32
    )


def on_device(
    pooled,
    routes,
    labels,
    in_weight,
    out_weight,
    gate_weight,
    tower_weight,
    tower_bias,
    bag_rows,
    bag_sample,
    bag_weight,
    row_table,
):
    owner_count = lax.axis_size("expert")
    tok_rows, feature = pooled.shape
    task_count = tower_weight.shape[0]
    hidden_width = in_weight.shape[1]
    capacity = 3 * tok_rows // owner_count
    slot_index = route_slots(routes, owner_count, capacity)
    in_matrix = in_weight[0]
    out_matrix = out_weight[0]
    paired = jnp.repeat(pooled, 2, axis=0)
    outbound = jnp.zeros((owner_count * capacity, feature), jnp.bfloat16).at[slot_index].set(paired)
    outbound = outbound.reshape(owner_count, capacity, feature)
    received = lax.all_to_all(outbound, "expert", split_axis=0, concat_axis=0, tiled=True)
    sources, slot_count, _ = received.shape
    expert_inputs = received.reshape(sources * slot_count, feature)
    pre_silu = contract_last(expert_inputs, in_matrix)
    expert_hidden_act = jax.nn.silu(pre_silu).astype(jnp.bfloat16)
    result = jnp.dot(expert_hidden_act, out_matrix, preferred_element_type=jnp.float32).astype(
        jnp.bfloat16
    )
    returned = lax.all_to_all(
        result.reshape(sources, slot_count, feature),
        "expert",
        split_axis=0,
        concat_axis=0,
        tiled=True,
    )
    returned, received, pre_stack = (
        returned,
        received,
        pre_silu.reshape(sources, slot_count, hidden_width),
    )
    expert_out = (
        returned.reshape(-1, feature)[slot_index].astype(jnp.float32).reshape(tok_rows, 2, feature)
    )
    experts_all = gate_weight.shape[0]
    one_hot = (
        routes[:, :, None] == jnp.arange(experts_all, dtype=jnp.int32)[None, None, :]
    ).astype(jnp.float32)
    gate_flat = gate_weight.reshape(experts_all * task_count, feature)
    all_logits = contract_last(pooled, gate_flat).reshape(tok_rows, experts_all, task_count)
    chosen = jnp.einsum("nke,net->ntk", one_hot, all_logits, precision=HIGH)
    gate_first = jax.nn.sigmoid(chosen[:, :, 0] - chosen[:, :, 1])
    gate_second = 1.0 - gate_first
    mixture = (
        gate_first[:, :, None] * expert_out[:, None, 0, :]
        + gate_second[:, :, None] * expert_out[:, None, 1, :]
    )
    task_logit = jnp.sum(mixture * tower_weight[None], axis=2) + tower_bias[None]
    logit_grad = LOSS_SCALE * (jax.nn.sigmoid(task_logit) - labels.astype(jnp.float32))
    tower_local = jnp.einsum("nt,ntf->tf", logit_grad, mixture, precision=HIGH)
    mixture_grad = logit_grad[:, :, None] * tower_weight[None]
    routed_grad = jnp.stack(
        [
            jnp.sum(gate_first[:, :, None] * mixture_grad, axis=1),
            jnp.sum(gate_second[:, :, None] * mixture_grad, axis=1),
        ],
        axis=1,
    ).astype(jnp.bfloat16)
    gate_dot = jnp.einsum("ntf,nkf->ntk", mixture_grad, expert_out, precision=HIGH)
    first_grad = (gate_dot[:, :, 0] - gate_dot[:, :, 1]) * gate_first * gate_second
    select_grad = jnp.stack([first_grad, -first_grad], axis=2)
    mix_table = jnp.einsum("nke,ntk->net", one_hot, select_grad, precision=HIGH).reshape(
        tok_rows, experts_all * task_count
    )
    gate_local = lax.dot_general(
        mix_table, pooled.astype(jnp.float32), (((0,), (0,)), ((), ())), precision=HIGH
    ).reshape(experts_all, task_count, feature)
    gate_input = jnp.dot(mix_table, gate_flat.astype(jnp.float32), precision=HIGH)
    grad_outbound = (
        jnp.zeros((owner_count * capacity, feature), jnp.bfloat16)
        .at[slot_index]
        .set(routed_grad.reshape(tok_rows * 2, feature))
    )
    grad_received = lax.all_to_all(
        grad_outbound.reshape(owner_count, capacity, feature),
        "expert",
        split_axis=0,
        concat_axis=0,
        tiled=True,
    )
    inputs = received.reshape(-1, feature)
    grad_rows = grad_received.reshape(-1, feature)
    pre_silu = pre_stack.reshape(-1, hidden_width)
    hidden_act = jax.nn.silu(pre_silu).astype(jnp.bfloat16)
    hidden_grad = contract_last(grad_rows, out_matrix)
    pre_grad = (hidden_grad * silu_grad(pre_silu)).astype(jnp.bfloat16)
    input_rows = jnp.dot(pre_grad, in_matrix, preferred_element_type=jnp.float32).astype(
        jnp.bfloat16
    )
    grad_back = lax.all_to_all(
        input_rows.reshape(owner_count, capacity, feature),
        "expert",
        split_axis=0,
        concat_axis=0,
        tiled=True,
    )
    input_grad = (
        grad_back.reshape(-1, feature)[slot_index].astype(jnp.float32).reshape(tok_rows, 2, feature)
    )
    pooled_grad = gate_input + input_grad[:, 0] + input_grad[:, 1]
    per_owner = bag_rows.shape[0] // owner_count
    row_grads = (
        (bag_weight[:, None] * pooled_grad[bag_sample])
        .astype(jnp.bfloat16)
        .reshape(owner_count, per_owner, feature)
    )
    owned_grads, owned_rows = (
        lax.all_to_all(row_grads, "expert", split_axis=0, concat_axis=0, tiled=True),
        lax.all_to_all(
            bag_rows.reshape(owner_count, per_owner),
            "expert",
            split_axis=0,
            concat_axis=0,
            tiled=True,
        ),
    )
    table_size = row_table.shape[0]
    summed = lax.psum_scatter(
        jnp.concatenate(
            [contract_first(pre_grad, inputs), contract_first(hidden_act, grad_rows)], axis=1
        ),
        "dp",
        scatter_dimension=0,
        tiled=True,
    )
    in_grad = summed[:, :feature][None]
    out_grad = summed[:, feature:][None]
    gate_total, tower_grad = lax.psum((gate_local, tower_local), ("expert", "dp"))
    gate_grad = lax.dynamic_slice_in_dim(gate_total, lax.axis_index("expert"), 1, 0)
    matches = (
        owned_rows.reshape(-1)[:, None] == jnp.arange(table_size, dtype=jnp.int32)[None, :]
    ).astype(jnp.bfloat16)
    row_sums = lax.psum(contract_first(matches, owned_grads.reshape(-1, feature)), "dp")
    new_table = row_table - STEP_SIZE * row_sums
    return (in_grad, out_grad, gate_grad, tower_grad, new_table)


def solution(mesh):
    in_specs = (
        P(("expert", "dp"), None),
        P(("expert", "dp"), None),
        P(("expert", "dp"), None),
        P("expert", None, None),
        P("expert", None, None),
        P(),
        P(),
        P(),
        P(("expert", "dp")),
        P(("expert", "dp")),
        P(("expert", "dp")),
        P("expert", None),
    )
    out_specs = (
        P("expert", "dp", None),
        P("expert", "dp", None),
        P("expert", None, None),
        P(),
        P("expert", None),
    )
    return jax.shard_map(
        on_device, mesh=mesh, in_specs=in_specs, out_specs=out_specs, check_vma=False
    )
```

profile of v0, /device:TPU:0, one launch (start us, length us, event | category | flops | bytes accessed | tf_op | source)
XLA Modules:
  0.0 216.7 jit_solution(16531580779659495678)
XLA Ops:
  7.2 0.8 broadcast_multiply_fusion
  8.0 0.8 copy.107
  9.4 1.2 reduce-window.6
  10.6 0.2 slice_reduce_fusion
  10.8 1.1 broadcast_in_dim.13
  12.1 3.1 %scatter_custom_fusion = bf16[768,256]{1,0:T(8,128)(2,1)} fusion(s32[512]{0:T(512)S(1)} %bitcast.112, bf16[512,256]{1,0:T(8,128)(2,1)S(1)} %reshape.166, bf16[]{:T(256)} %constant.13.clone.1), kind=kCustom, calls=%fused_computation.51 | custom fusion | bytes 393218 | tf_op jit(solution)/shard_map/scatter | solution.py:59
  15.2 8.3 %all-to-all-start = ((bf16[16,48,256]{2,1,0:T(8,128)(2,1)}), bf16[16,48,256]{2,1,0:T(8,128)(2,1)S(1)}, u32[]{:S(2)}, u32[]{:S(2)}) async-start(bf16[16,48,256]{2,1,0:T(8,128)(2,1)} %bitcast.5), calls=%async_computation | async-start | bytes 786432 | tf_op jit(solution)/shard_map/all_to_all | solution.py:61
  23.5 1.1 fusion.34
  24.6 0.2 copy.112
  24.8 11.4 %all-to-all-done = bf16[16,48,256]{2,1,0:T(8,128)(2,1)S(1)} async-done(((bf16[16,48,256]{2,1,0:T(8,128)(2,1)}), bf16[16,48,256]{2,1,0:T(8,128)(2,1)S(1)}, u32[]{:S(2)}, u32[]{:S(2)}) %all-to-all-start) | async-done | bytes 393248 | tf_op jit(solution)/shard_map/all_to_all | solution.py:61
  36.1 6.5 %multiply_convert_fusion.1 = (bf16[768,4096]{1,0:T(8,128)(2,1)S(1)}, f32[768,4096]{1,0:T(8,128)}) fusion(bf16[768,256]{1,0:T(8,128)(2,1)S(1)} %bitcast.101, bf16[1,4096,256]{2,1,0:T(8,128)(2,1)S(1)} %copy-done), kind=kOutput, calls=%fused_computation.6 | convolution fusion | flops 1626341376 | bytes 21364736 | tf_op jit(solution)/shard_map/dot_general | solution.py:31
  42.6 2.6 %copy-done.2 = bf16[768,4096]{1,0:T(8,128)(2,1)} copy-done((bf16[768,4096]{1,0:T(8,128)(2,1)}, bf16[768,4096]{1,0:T(8,128)(2,1)S(1)}, u32[]{:S(2)}) %copy-start.2) | copy-done | bytes 6291480
  45.2 2.5 %fusion.11 = bf16[768,256]{1,0:T(8,128)(2,1)} fusion(bf16[768,4096]{1,0:T(8,128)(2,1)S(1)} %get-tuple-element.55, bf16[1,4096,256]{2,1,0:T(8,128)(2,1)S(1)} %copy-done.23), kind=kOutput, calls=%fused_computation.21 | convolution fusion | flops 1610809344 | bytes 8781824 | tf_op jit(solution)/shard_map/dot_general | solution.py:66
  47.8 3.7 %all-to-all-start.1 = ((bf16[16,48,256]{2,1,0:T(8,128)(2,1)}), bf16[16,48,256]{2,1,0:T(8,128)(2,1)S(1)}, u32[]{:S(2)}, u32[]{:S(2)}) async-start(bf16[16,48,256]{2,1,0:T(8,128)(2,1)} %bitcast.9), calls=%async_computation.1 | async-start | bytes 786432 | tf_op jit(solution)/shard_map/all_to_all | solution.py:69
  51.5 1.1 fusion.27
  52.6 0.2 fusion.50
  53.3 0.7 all_to_all.24
  54.0 9.5 %all-to-all-done.1 = bf16[16,48,256]{2,1,0:T(8,128)(2,1)S(1)} async-done(((bf16[16,48,256]{2,1,0:T(8,128)(2,1)}), bf16[16,48,256]{2,1,0:T(8,128)(2,1)S(1)}, u32[]{:S(2)}, u32[]{:S(2)}) %all-to-all-start.1) | async-done | bytes 393248 | tf_op jit(solution)/shard_map/all_to_all | solution.py:69
  63.6 3.7 %all-to-all-start.3 = ((s32[16,1,32]{2,1,0:T(1,128)}), s32[16,1,32]{2,1,0:T(1,128)S(1)}, u32[]{:S(2)}, u32[]{:S(2)}) async-start(s32[16,1,32]{2,1,0:T(1,128)} %all_to_all.24), calls=%async_computation.4 | async-start | bytes 16384 | tf_op jit(solution)/shard_map/all_to_all | solution.py:158
  67.3 2.0 gather_fusion
  69.3 0.4 fusion.49
  69.8 1.2 multiply_reduce_fusion
  71.3 1.6 fusion.19
  72.9 1.0 copy.119
  73.9 1.1 reshape.174
  74.9 3.1 %scatter_custom_fusion.1 = bf16[768,256]{1,0:T(8,128)(2,1)} fusion(s32[512]{0:T(512)S(1)} %bitcast.114, bf16[512,256]{1,0:T(8,128)(2,1)S(1)} %reshape.174, bf16[]{:T(256)} %constant.13.clone.1), kind=kCustom, calls=%fused_computation.49 | custom fusion | bytes 393218 | tf_op jit(solution)/shard_map/scatter | solution.py:121
  78.0 0.6 copy-done.10
  78.6 6.8 %all-to-all-start.2 = ((bf16[16,48,256]{2,1,0:T(8,128)(2,1)}), bf16[16,48,256]{2,1,0:T(8,128)(2,1)S(1)}, u32[]{:S(2)}, u32[]{:S(2)}) async-start(bf16[16,48,256]{2,1,0:T(8,128)(2,1)} %bitcast.14), calls=%async_computation.2 | async-start | bytes 786432 | tf_op jit(solution)/shard_map/all_to_all | solution.py:123
  85.5 0.8 mul.155
  86.2 0.7 compare_select_fusion.1
  86.9 0.6 pad_clamp_fusion
  87.5 0.5 broadcast.113
  88.0 1.3 reduce.5
  89.3 0.7 eq.64
  90.0 2.7 %fusion.17 = f32[256,2,2]{1,2,0:T(2,128)} fusion(bf16[256,2,256]{2,1,0:T(2,128)(2,1)S(1)} %gather.14, f32[256,2]{1,0:T(8,128)S(1)} %copy.118, f32[2,256]{1,0:T(2,128)} %param.18), kind=kOutput, calls=%fused_computation.27 | convolution fusion | flops 3276800 | bytes 270336 | tf_op jit(solution)/shard_map/ntf,nkf->ntk/dot_general | solution.py:108
  92.6 3.9 %all-to-all-done.2 = bf16[16,48,256]{2,1,0:T(8,128)(2,1)S(1)} async-done(((bf16[16,48,256]{2,1,0:T(8,128)(2,1)}), bf16[16,48,256]{2,1,0:T(8,128)(2,1)S(1)}, u32[]{:S(2)}, u32[]{:S(2)}) %all-to-all-start.2) | async-done | bytes 393248 | tf_op jit(solution)/shard_map/all_to_all | solution.py:123
  96.6 8.8 %multiply_convert_fusion = bf16[768,4096]{1,0:T(8,128)(2,1)S(1)} fusion(f32[768,4096]{1,0:T(8,128)} %get-tuple-element.56, bf16[768,256]{1,0:T(8,128)(2,1)S(1)} %bitcast.103, bf16[1,4096,256]{2,1,0:T(8,128)(2,1)} %param.16), kind=kOutput, calls=%fused_computation.5 | convolution fusion | flops 1638924288 | bytes 21364736 | tf_op jit(solution)/shard_map/dot_general | solution.py:31
  105.3 2.7 %copy-done.3 = bf16[768,4096]{1,0:T(8,128)(2,1)} copy-done((bf16[768,4096]{1,0:T(8,128)(2,1)}, bf16[768,4096]{1,0:T(8,128)(2,1)S(1)}, u32[]{:S(2)}) %copy-start.3) | copy-done | bytes 6291480
  108.0 2.5 %fusion.8 = bf16[768,256]{1,0:T(8,128)(2,1)} fusion(bf16[768,4096]{1,0:T(8,128)(2,1)S(1)} %multiply_convert_fusion, bf16[1,4096,256]{2,1,0:T(8,128)(2,1)S(1)} %copy-done), kind=kOutput, calls=%fused_computation.20 | convolution fusion | flops 1610809344 | bytes 8781824 | tf_op jit(solution)/shard_map/dot_general | solution.py:136
  110.5 3.9 %all-to-all-start.4 = ((bf16[16,48,256]{2,1,0:T(8,128)(2,1)}), bf16[16,48,256]{2,1,0:T(8,128)(2,1)S(1)}, u32[]{:S(2)}, u32[]{:S(2)}) async-start(bf16[16,48,256]{2,1,0:T(8,128)(2,1)} %bitcast.107), calls=%async_computation.5 | async-start | bytes 786432 | tf_op jit(solution)/shard_map/all_to_all | solution.py:139
  114.5 1.3 fusion.48
  116.1 1.8 fusion.26
  117.9 7.9 %all-to-all-done.4 = bf16[16,48,256]{2,1,0:T(8,128)(2,1)S(1)} async-done(((bf16[16,48,256]{2,1,0:T(8,128)(2,1)}), bf16[16,48,256]{2,1,0:T(8,128)(2,1)S(1)}, u32[]{:S(2)}, u32[]{:S(2)}) %all-to-all-start.4) | async-done | bytes 393248 | tf_op jit(solution)/shard_map/all_to_all | solution.py:139
  125.8 1.9 gather_fusion.1
  127.8 0.3 reshape.137
  128.0 0.4 fusion.47
  128.5 1.3 fusion.15
  129.8 1.6 gather_fusion.2
  131.3 0.8 multiply_convert_fusion.2
  132.2 3.6 %all-to-all-start.5 = ((bf16[16,32,256]{2,1,0:T(8,128)(2,1)}), bf16[16,32,256]{2,1,0:T(8,128)(2,1)S(1)}, u32[]{:S(2)}, u32[]{:S(2)}) async-start(bf16[16,32,256]{2,1,0:T(8,128)(2,1)} %multiply_convert_fusion.2), calls=%async_computation.6 | async-start | bytes 524288 | tf_op jit(solution)/shard_map/all_to_all | solution.py:157
  135.9 6.7 %fusion.52 = f32[4096,256]{0,1:T(8,128)} fusion(bf16[768,4096]{1,0:T(8,128)(2,1)} %copy-done.2, bf16[768,256]{1,0:T(8,128)(2,1)} %bitcast.104), kind=kOutput, calls=%fused_computation.92 | convolution fusion | flops 1610612736 | bytes 10878976 | tf_op jit(solution)/shard_map/dot_general | solution.py:25
  142.6 2.1 all-to-all-done.5
  144.7 1.8 fusion.7
  146.6 4.8 %fusion.51 = f32[4096,256]{0,1:T(8,128)S(1)} fusion(bf16[768,4096]{1,0:T(8,128)(2,1)} %copy-done.3, bf16[768,256]{1,0:T(8,128)(2,1)S(1)} %bitcast.102), kind=kOutput, calls=%fused_computation.91 | convolution fusion | flops 1610612736 | bytes 10878976 | tf_op jit(solution)/shard_map/dot_general | solution.py:25
  151.4 3.8 %pad_maximum_fusion = f32[4096,512]{0,1:T(8,128)} fusion(f32[4096,256]{0,1:T(8,128)S(1)} %copy-done.1, f32[4096,256]{0,1:T(8,128)S(1)} %fusion.51), kind=kLoop, calls=%fused_computation.8 | loop fusion | flops 2097152 | bytes 16777216 | tf_op jit(solution)/shard_map/concatenate | solution.py:168
  155.2 0.9 copy-done.8
  156.3 0.4 fusion.21
  156.7 0.2 fusion.32
  156.9 39.3 %all-reduce = (f32[16,2,256]{2,0,1:T(8,128)S(1)}, f32[2,256]{1,0:T(2,128)}) all-reduce(f32[16,2,256]{2,0,1:T(8,128)S(1)} %fusion.32, f32[2,256]{1,0:T(2,128)S(1)} %bitcast.116), channel_id=1, replica_groups=mesh['expert'=16,'dp'=2] {'expert','dp'}, use_global_device_ids=true, to_apply=%region_9.10 | all-reduce | flops 8704 | bytes 69632 | tf_op jit(solution)/shard_map/psum | solution.py:177
  196.2 0.6 copy.131
  196.8 2.6 %multiply_subtract_fusion = f32[1024,256]{1,0:T(8,128)} fusion(f32[1024,256]{1,0:T(8,128)} %param.23, f32[1024,256]{1,0:T(8,128)} %all-reduce.3.cloned.1.call-done), kind=kLoop, calls=%fused_computation.25 | loop fusion | flops 524288 | bytes 3145728 | tf_op jit(solution)/shard_map/sub | solution.py:183
  199.4 4.7 %slice_bitcast_fusion = (f32[1,2048,256]{1,2,0:T(8,128)}, f32[1,2048,256]{1,2,0:T(8,128)}) fusion(f32[2048,512]{0,1:T(8,128)} %reduce-scatter.2.cloned.1.call-done), kind=kLoop, calls=%fused_computation.9 | loop fusion | bytes 8388608 | tf_op jit(solution)/shard_map/broadcast_in_dim | solution.py:176
  204.1 2.9 %copy.129 = f32[1,2048,256]{2,1,0:T(8,128)} copy(f32[1,2048,256]{1,2,0:T(8,128)} %get-tuple-element.46) | data formatting | bytes 4194304
  207.0 2.9 %copy.130 = f32[1,2048,256]{2,1,0:T(8,128)} copy(f32[1,2048,256]{1,2,0:T(8,128)} %get-tuple-element.45) | data formatting | bytes 4194304
  (83 shorter events, 2.5 us)
Async XLA Ops:
  7.2 29.0 %copy-start = (bf16[1,4096,256]{2,1,0:T(8,128)(2,1)S(1)}, bf16[1,4096,256]{2,1,0:T(8,128)(2,1)}, u32[]{:S(2)}) copy-start(bf16[1,4096,256]{2,1,0:T(8,128)(2,1)} %param.15) | copy-start | bytes 6291460
  15.2 21.0 %all-to-all-start = ((bf16[16,48,256]{2,1,0:T(8,128)(2,1)}), bf16[16,48,256]{2,1,0:T(8,128)(2,1)S(1)}, u32[]{:S(2)}, u32[]{:S(2)}) async-start(bf16[16,48,256]{2,1,0:T(8,128)(2,1)} %bitcast.5), calls=%async_computation | async-start | bytes 786432 | tf_op jit(solution)/shard_map/all_to_all | solution.py:61
  36.1 6.5 %copy-start.4 = (bf16[16,48,256]{2,1,0:T(8,128)(2,1)}, bf16[16,48,256]{2,1,0:T(8,128)(2,1)S(1)}, u32[]{:S(2)}) copy-start(bf16[16,48,256]{2,1,0:T(8,128)(2,1)S(1)} %all-to-all-done) | copy-start | bytes 1179652
  36.1 9.1 %copy-start.23 = (bf16[1,4096,256]{2,1,0:T(8,128)(2,1)S(1)}, bf16[1,4096,256]{2,1,0:T(8,128)(2,1)}, u32[]{:S(2)}) copy-start(bf16[1,4096,256]{2,1,0:T(8,128)(2,1)} %param.16) | copy-start | bytes 6291460
  42.6 2.6 %copy-start.2 = (bf16[768,4096]{1,0:T(8,128)(2,1)}, bf16[768,4096]{1,0:T(8,128)(2,1)S(1)}, u32[]{:S(2)}) copy-start(bf16[768,4096]{1,0:T(8,128)(2,1)S(1)} %get-tuple-element.55) | copy-start | bytes 18874372
  45.2 8.1 %copy-start.19 = (s32[512]{0:T(512)S(1)}, s32[512]{0:T(512)}, u32[]{:S(2)}) copy-start(s32[512]{0:T(512)} %param.20) | copy-start | bytes 6148
  47.8 22.0 %copy-start.18 = (f32[2,256]{1,0:T(2,128)S(1)}, f32[2,256]{1,0:T(2,128)}, u32[]{:S(2)}) copy-start(f32[2,256]{1,0:T(2,128)} %param.18) | copy-start | bytes 6148
  47.8 23.3 %copy-start.21 = (s32[256,2]{0,1:T(2,128)S(1)}, s32[256,2]{0,1:T(2,128)}, u32[]{:S(2)}) copy-start(s32[256,2]{0,1:T(2,128)} %param.14) | copy-start | bytes 6148
  47.8 23.3 %copy-start.22 = (f32[2]{0:T(128)S(1)}, f32[2]{0:T(128)}, u32[]{:S(2)}) copy-start(f32[2]{0:T(128)} %param.19) | copy-start | bytes 28
  47.8 15.8 %all-to-all-start.1 = ((bf16[16,48,256]{2,1,0:T(8,128)(2,1)}), bf16[16,48,256]{2,1,0:T(8,128)(2,1)S(1)}, u32[]{:S(2)}, u32[]{:S(2)}) async-start(bf16[16,48,256]{2,1,0:T(8,128)(2,1)} %bitcast.9), calls=%async_computation.1 | async-start | bytes 786432 | tf_op jit(solution)/shard_map/all_to_all | solution.py:69
  53.0 14.2 %copy-start.13 = (f32[256,2,1]{0,1,2:T(2,128)}, f32[256,2,1]{0,1,2:T(2,128)S(1)}, u32[]{:S(2)}) copy-start(f32[256,2,1]{0,1,2:T(2,128)S(1)} %get-tuple-element.44) | copy-start | bytes 6148
  54.0 15.7 %copy-start.15 = (s32[1024]{0:T(1024)}, s32[1024]{0:T(1024)S(1)}, u32[]{:S(2)}) copy-start(s32[1024]{0:T(1024)S(1)} %pad_clamp_fusion.1) | copy-start | bytes 12292
  63.6 14.4 %all-to-all-start.3 = ((s32[16,1,32]{2,1,0:T(1,128)}), s32[16,1,32]{2,1,0:T(1,128)S(1)}, u32[]{:S(2)}, u32[]{:S(2)}) async-start(s32[16,1,32]{2,1,0:T(1,128)} %all_to_all.24), calls=%async_computation.4 | async-start | bytes 16384 | tf_op jit(solution)/shard_map/all_to_all | solution.py:158
  71.1 1.7 copy-start.11
  78.0 0.6 copy-start.10
  78.6 18.0 %all-to-all-start.2 = ((bf16[16,48,256]{2,1,0:T(8,128)(2,1)}), bf16[16,48,256]{2,1,0:T(8,128)(2,1)S(1)}, u32[]{:S(2)}, u32[]{:S(2)}) async-start(bf16[16,48,256]{2,1,0:T(8,128)(2,1)} %bitcast.14), calls=%async_computation.2 | async-start | bytes 786432 | tf_op jit(solution)/shard_map/all_to_all | solution.py:123
  96.6 8.8 %copy-start.6 = (bf16[16,48,256]{2,1,0:T(8,128)(2,1)}, bf16[16,48,256]{2,1,0:T(8,128)(2,1)S(1)}, u32[]{:S(2)}) copy-start(bf16[16,48,256]{2,1,0:T(8,128)(2,1)S(1)} %all-to-all-done.2) | copy-start | bytes 1179652
  105.3 2.7 %copy-start.3 = (bf16[768,4096]{1,0:T(8,128)(2,1)}, bf16[768,4096]{1,0:T(8,128)(2,1)S(1)}, u32[]{:S(2)}) copy-start(bf16[768,4096]{1,0:T(8,128)(2,1)S(1)} %multiply_convert_fusion) | copy-start | bytes 18874372
  108.0 7.9 %copy-start.14 = (f32[256,2,1]{0,1,2:T(2,128)S(1)}, f32[256,2,1]{0,1,2:T(2,128)}, u32[]{:S(2)}) copy-start(f32[256,2,1]{0,1,2:T(2,128)} %copy-done.13) | copy-start | bytes 6148
  108.0 17.8 %copy-start.16 = (s32[1024]{0:T(1024)S(1)}, s32[1024]{0:T(1024)}, u32[]{:S(2)}) copy-start(s32[1024]{0:T(1024)} %copy-done.15) | copy-start | bytes 12292
  110.5 17.9 %copy-start.9 = (bf16[16,2,256]{2,1,0:T(2,128)(2,1)S(1)}, bf16[16,2,256]{2,1,0:T(2,128)(2,1)}, u32[]{:S(2)}) copy-start(bf16[16,2,256]{2,1,0:T(2,128)(2,1)} %param.17) | copy-start | bytes 49156
  110.5 19.2 %copy-start.17 = (s32[1024]{0:T(1024)S(1)}, s32[1024]{0:T(1024)}, u32[]{:S(2)}) copy-start(s32[1024]{0:T(1024)} %pad_clamp_fusion) | copy-start | bytes 12292
  110.5 15.3 %all-to-all-start.4 = ((bf16[16,48,256]{2,1,0:T(8,128)(2,1)}), bf16[16,48,256]{2,1,0:T(8,128)(2,1)S(1)}, u32[]{:S(2)}, u32[]{:S(2)}) async-start(bf16[16,48,256]{2,1,0:T(8,128)(2,1)} %bitcast.107), calls=%async_computation.5 | async-start | bytes 786432 | tf_op jit(solution)/shard_map/all_to_all | solution.py:139
  132.2 12.5 %all-to-all-start.5 = ((bf16[16,32,256]{2,1,0:T(8,128)(2,1)}), bf16[16,32,256]{2,1,0:T(8,128)(2,1)S(1)}, u32[]{:S(2)}, u32[]{:S(2)}) async-start(bf16[16,32,256]{2,1,0:T(8,128)(2,1)} %multiply_convert_fusion.2), calls=%async_computation.6 | async-start | bytes 524288 | tf_op jit(solution)/shard_map/all_to_all | solution.py:157
  135.8 8.9 %copy-start.20 = (s32[512]{0:T(512)S(1)}, s32[512]{0:T(512)}, u32[]{:S(2)}) copy-start(s32[512]{0:T(512)} %eq.64) | copy-start | bytes 6148
  135.8 10.7 %copy-start.5 = (bf16[16,48,256]{2,1,0:T(8,128)(2,1)S(1)}, bf16[16,48,256]{2,1,0:T(8,128)(2,1)}, u32[]{:S(2)}) copy-start(bf16[16,48,256]{2,1,0:T(8,128)(2,1)} %copy-done.4) | copy-start | bytes 1179652
  135.8 60.9 %all-reduce.3.cloned.1.call-start = ((), (), s32[]{:S(2)}) async-start(), calls=%async_computation.8 | async-start | bytes 2097152 | tf_op jit(solution)/shard_map/psum | solution.py:182
  146.5 52.9 %reduce-scatter.2.cloned.1.call-start = ((), (), s32[]{:S(2)}) async-start(), calls=%async_computation.7 | async-start | bytes 12582912 | tf_op jit(solution)/shard_map/reduce_scatter | solution.py:167
  146.6 4.8 %copy-start.1 = (f32[4096,256]{0,1:T(8,128)S(1)}, f32[4096,256]{0,1:T(8,128)}, u32[]{:S(2)}) copy-start(f32[4096,256]{0,1:T(8,128)} %fusion.52) | copy-start | bytes 12582916
  155.2 0.9 copy-start.8
  155.2 1.1 copy-start.12
  155.2 1.5 copy-start.7
Sparse Core Ops, SparseCore 0:
  146.6 18.6 all-reduce.2
  167.6 17.4 reduce-scatter.1
where the time goes:
time: 218 us; the launch traced here: 217 us
  matrix products  42.1 us (19%)
  local copies, waits for them, and re-layouts  40.9 us (19%)
  blocking collectives  39.3 us (18%)
  waiting for transfers between devices  34.8 us (16%)
  starting transfers between devices  30.2 us (14%)
  other arithmetic  14.8 us (7%)
  between operations  14.5 us (7%)
    psum x1, blocking collectives, on_device(): lax.psum((gate_local, tower_local), ('expert', 'dp'))  39.3 us
    dot_general x3, matrix products, contract_last(): lax.dot_general(left, right, (((1,), (1,)), ((), ())), preferred_element_...  16.3 us
    unnamed x57, local copies, waits for them, and re-layouts  14.4 us
    dot_general x3, matrix products, contract_first(): lax.dot_general(left, right, (((0,), (0,)), ((), ())), preferred_element_...  13.3 us
    all_to_all x1, waiting for transfers between devices, on_device(): lax.all_to_all(outbound, 'expert', split_axis=0, concat_axis=0, tiled=True)  11.4 us
    all_to_all x1, waiting for transfers between devices, on_device(): lax.all_to_all(result.reshape(sources, slot_count, feature), 'expert', sp...  9.54 us
    all_to_all x1, starting transfers between devices, on_device(): lax.all_to_all(outbound, 'expert', split_axis=0, concat_axis=0, tiled=True)  8.34 us
    all_to_all x1, waiting for transfers between devices, on_device(): lax.all_to_all(input_rows.reshape(owner_count, capacity, feature), 'exper...  7.88 us
  transfers between devices with their start and end apart: 8, of which 5 were waited for; matrix products, arithmetic and copies ran while one was open for 20% of the time, Pallas kernels for 0%

commit v1 on v0

--- a/solution.py
+++ b/solution.py
@@ -174,7 +174,13 @@
     )
     in_grad = summed[:, :feature][None]
     out_grad = summed[:, feature:][None]
-    gate_total, tower_grad = lax.psum((gate_local, tower_local), ("expert", "dp"))
+
+    def trace_digits(payload, ax_name, device_axis):
+        for dev_j in (ax_name, device_axis):
+            payload = lax.psum(payload, axis_name=dev_j)
+        return payload
+
+    gate_total, tower_grad = trace_digits((gate_local, tower_local), "dp", "expert")
     gate_grad = lax.dynamic_slice_in_dim(gate_total, lax.axis_index("expert"), 1, 0)
     matches = (
         owned_rows.reshape(-1)[:, None] == jnp.arange(table_size, dtype=jnp.int32)[None, :]

time: 218 us -> 258 us (1.18)
  blocking collectives: 39.3 us -> 79.1 us
    psum x1 -> x2, blocking collectives: 39.3 us -> 79.1 us  [trace_digits(): payload = lax.psum(payload, axis_name=dev_j)]
  transfers between devices with their start and end apart: 8 -> 8, of which waited for: 5 -> 5; matrix products, arithmetic and copies ran while one was open for 20% -> 17% of each run, Pallas kernels for 0% -> 0%
where the time goes in v1:
time: 258 us; the launch traced here: 257 us
  blocking collectives  79.1 us (31%)
  matrix products  42.1 us (16%)
  local copies, waits for them, and re-layouts  40.9 us (16%)
  waiting for transfers between devices  34.8 us (13%)
  starting transfers between devices  30.2 us (12%)
  other arithmetic  14.9 us (6%)
  between operations  14.5 us (6%)
    psum x2, blocking collectives, trace_digits(): payload = lax.psum(payload, axis_name=dev_j)  79.1 us
    dot_general x3, matrix products, contract_last(): lax.dot_general(left, right, (((1,), (1,)), ((), ())), preferred_element_...  16.3 us
    unnamed x57, local copies, waits for them, and re-layouts  14.3 us
    dot_general x3, matrix products, contract_first(): lax.dot_general(left, right, (((0,), (0,)), ((), ())), preferred_element_...  13.3 us
    all_to_all x1, waiting for transfers between devices, on_device(): lax.all_to_all(outbound, 'expert', split_axis=0, concat_axis=0, tiled=True)  11.4 us
    all_to_all x1, waiting for transfers between devices, on_device(): lax.all_to_all(result.reshape(sources, slot_count, feature), 'expert', sp...  9.54 us
    all_to_all x1, starting transfers between devices, on_device(): lax.all_to_all(outbound, 'expert', split_axis=0, concat_axis=0, tiled=True)  8.34 us
    all_to_all x1, waiting for transfers between devices, on_device(): lax.all_to_all(input_rows.reshape(owner_count, capacity, feature), 'exper...  7.89 us
  transfers between devices with their start and end apart: 8, of which 5 were waited for; matrix products, arithmetic and copies ran while one was open for 17% of the time, Pallas kernels for 0%

profile of v1, /device:TPU:0, one launch (start us, length us, event | category | flops | bytes accessed | tf_op | source)
XLA Modules:
  0.0 256.5 jit_solution(5008889264816080463)
XLA Ops:
  7.2 0.8 broadcast_multiply_fusion
  8.0 0.8 copy.107
  9.4 1.2 reduce-window.6
  10.6 0.2 slice_reduce_fusion
  10.8 1.1 broadcast_in_dim.13
  12.1 3.1 %scatter_custom_fusion = bf16[768,256]{1,0:T(8,128)(2,1)} fusion(s32[512]{0:T(512)S(1)} %bitcast.112, bf16[512,256]{1,0:T(8,128)(2,1)S(1)} %reshape.166, bf16[]{:T(256)} %constant.13.clone.1), kind=kCustom, calls=%fused_computation.51 | custom fusion | bytes 393218 | tf_op jit(solution)/shard_map/scatter | solution.py:59
  15.2 8.3 %all-to-all-start = ((bf16[16,48,256]{2,1,0:T(8,128)(2,1)}), bf16[16,48,256]{2,1,0:T(8,128)(2,1)S(1)}, u32[]{:S(2)}, u32[]{:S(2)}) async-start(bf16[16,48,256]{2,1,0:T(8,128)(2,1)} %bitcast.5), calls=%async_computation | async-start | bytes 786432 | tf_op jit(solution)/shard_map/all_to_all | solution.py:61
  23.5 1.1 fusion.34
  24.8 11.4 %all-to-all-done = bf16[16,48,256]{2,1,0:T(8,128)(2,1)S(1)} async-done(((bf16[16,48,256]{2,1,0:T(8,128)(2,1)}), bf16[16,48,256]{2,1,0:T(8,128)(2,1)S(1)}, u32[]{:S(2)}, u32[]{:S(2)}) %all-to-all-start) | async-done | bytes 393248 | tf_op jit(solution)/shard_map/all_to_all | solution.py:61
  36.1 6.5 %multiply_convert_fusion.1 = (bf16[768,4096]{1,0:T(8,128)(2,1)S(1)}, f32[768,4096]{1,0:T(8,128)}) fusion(bf16[768,256]{1,0:T(8,128)(2,1)S(1)} %bitcast.101, bf16[1,4096,256]{2,1,0:T(8,128)(2,1)S(1)} %copy-done), kind=kOutput, calls=%fused_computation.6 | convolution fusion | flops 1626341376 | bytes 21364736 | tf_op jit(solution)/shard_map/dot_general | solution.py:31
  42.6 2.6 %copy-done.2 = bf16[768,4096]{1,0:T(8,128)(2,1)} copy-done((bf16[768,4096]{1,0:T(8,128)(2,1)}, bf16[768,4096]{1,0:T(8,128)(2,1)S(1)}, u32[]{:S(2)}) %copy-start.2) | copy-done | bytes 6291480
  45.2 2.5 fusion.11
  47.7 3.7 %all-to-all-start.1 = ((bf16[16,48,256]{2,1,0:T(8,128)(2,1)}), bf16[16,48,256]{2,1,0:T(8,128)(2,1)S(1)}, u32[]{:S(2)}, u32[]{:S(2)}) async-start(bf16[16,48,256]{2,1,0:T(8,128)(2,1)} %bitcast.9), calls=%async_computation.1 | async-start | bytes 786432 | tf_op jit(solution)/shard_map/all_to_all | solution.py:69
  51.5 1.1 fusion.27
  52.6 0.2 fusion.50
  53.3 0.7 all_to_all.24
  54.0 9.5 %all-to-all-done.1 = bf16[16,48,256]{2,1,0:T(8,128)(2,1)S(1)} async-done(((bf16[16,48,256]{2,1,0:T(8,128)(2,1)}), bf16[16,48,256]{2,1,0:T(8,128)(2,1)S(1)}, u32[]{:S(2)}, u32[]{:S(2)}) %all-to-all-start.1) | async-done | bytes 393248 | tf_op jit(solution)/shard_map/all_to_all | solution.py:69
  63.5 3.7 %all-to-all-start.3 = ((s32[16,1,32]{2,1,0:T(1,128)}), s32[16,1,32]{2,1,0:T(1,128)S(1)}, u32[]{:S(2)}, u32[]{:S(2)}) async-start(s32[16,1,32]{2,1,0:T(1,128)} %all_to_all.24), calls=%async_computation.4 | async-start | bytes 16384 | tf_op jit(solution)/shard_map/all_to_all | solution.py:158
  67.2 2.0 gather_fusion
  69.3 0.4 fusion.49
  69.7 1.2 multiply_reduce_fusion
  71.2 1.6 fusion.19
  72.9 1.0 copy.119
  73.8 1.1 reshape.174
  74.9 3.1 %scatter_custom_fusion.1 = bf16[768,256]{1,0:T(8,128)(2,1)} fusion(s32[512]{0:T(512)S(1)} %bitcast.114, bf16[512,256]{1,0:T(8,128)(2,1)S(1)} %reshape.174, bf16[]{:T(256)} %constant.13.clone.1), kind=kCustom, calls=%fused_computation.49 | custom fusion | bytes 393218 | tf_op jit(solution)/shard_map/scatter | solution.py:121
  78.0 0.6 copy-done.10
  78.6 6.8 %all-to-all-start.2 = ((bf16[16,48,256]{2,1,0:T(8,128)(2,1)}), bf16[16,48,256]{2,1,0:T(8,128)(2,1)S(1)}, u32[]{:S(2)}, u32[]{:S(2)}) async-start(bf16[16,48,256]{2,1,0:T(8,128)(2,1)} %bitcast.14), calls=%async_computation.2 | async-start | bytes 786432 | tf_op jit(solution)/shard_map/all_to_all | solution.py:123
  85.4 0.8 mul.155
  86.2 0.7 compare_select_fusion.1
  86.9 0.6 pad_clamp_fusion
  87.5 0.5 broadcast.113
  88.0 1.3 reduce.5
  89.3 0.7 eq.64
  90.0 2.6 %fusion.17 = f32[256,2,2]{1,2,0:T(2,128)} fusion(bf16[256,2,256]{2,1,0:T(2,128)(2,1)S(1)} %gather.14, f32[256,2]{1,0:T(8,128)S(1)} %copy.118, f32[2,256]{1,0:T(2,128)} %param.18), kind=kOutput, calls=%fused_computation.27 | convolution fusion | flops 3276800 | bytes 270336 | tf_op jit(solution)/shard_map/ntf,nkf->ntk/dot_general | solution.py:108
  92.6 3.9 %all-to-all-done.2 = bf16[16,48,256]{2,1,0:T(8,128)(2,1)S(1)} async-done(((bf16[16,48,256]{2,1,0:T(8,128)(2,1)}), bf16[16,48,256]{2,1,0:T(8,128)(2,1)S(1)}, u32[]{:S(2)}, u32[]{:S(2)}) %all-to-all-start.2) | async-done | bytes 393248 | tf_op jit(solution)/shard_map/all_to_all | solution.py:123
  96.5 8.8 %multiply_convert_fusion = bf16[768,4096]{1,0:T(8,128)(2,1)S(1)} fusion(f32[768,4096]{1,0:T(8,128)} %get-tuple-element.58, bf16[768,256]{1,0:T(8,128)(2,1)S(1)} %bitcast.103, bf16[1,4096,256]{2,1,0:T(8,128)(2,1)} %param.16), kind=kOutput, calls=%fused_computation.5 | convolution fusion | flops 1638924288 | bytes 21364736 | tf_op jit(solution)/shard_map/dot_general | solution.py:31
  105.3 2.6 %copy-done.3 = bf16[768,4096]{1,0:T(8,128)(2,1)} copy-done((bf16[768,4096]{1,0:T(8,128)(2,1)}, bf16[768,4096]{1,0:T(8,128)(2,1)S(1)}, u32[]{:S(2)}) %copy-start.3) | copy-done | bytes 6291480
  108.0 2.5 fusion.8
  110.5 3.9 %all-to-all-start.4 = ((bf16[16,48,256]{2,1,0:T(8,128)(2,1)}), bf16[16,48,256]{2,1,0:T(8,128)(2,1)S(1)}, u32[]{:S(2)}, u32[]{:S(2)}) async-start(bf16[16,48,256]{2,1,0:T(8,128)(2,1)} %bitcast.107), calls=%async_computation.5 | async-start | bytes 786432 | tf_op jit(solution)/shard_map/all_to_all | solution.py:139
  114.4 1.3 fusion.48
  116.1 1.8 fusion.26
  117.9 7.9 %all-to-all-done.4 = bf16[16,48,256]{2,1,0:T(8,128)(2,1)S(1)} async-done(((bf16[16,48,256]{2,1,0:T(8,128)(2,1)}), bf16[16,48,256]{2,1,0:T(8,128)(2,1)S(1)}, u32[]{:S(2)}, u32[]{:S(2)}) %all-to-all-start.4) | async-done | bytes 393248 | tf_op jit(solution)/shard_map/all_to_all | solution.py:139
  125.8 1.9 gather_fusion.1
  127.7 0.3 reshape.137
  128.0 0.4 fusion.47
  128.4 1.3 fusion.15
  129.7 1.6 gather_fusion.2
  131.3 0.8 multiply_convert_fusion.2
  132.1 3.6 %all-to-all-start.5 = ((bf16[16,32,256]{2,1,0:T(8,128)(2,1)}), bf16[16,32,256]{2,1,0:T(8,128)(2,1)S(1)}, u32[]{:S(2)}, u32[]{:S(2)}) async-start(bf16[16,32,256]{2,1,0:T(8,128)(2,1)} %multiply_convert_fusion.2), calls=%async_computation.6 | async-start | bytes 524288 | tf_op jit(solution)/shard_map/all_to_all | solution.py:157
  135.9 6.7 %fusion.52 = f32[4096,256]{0,1:T(8,128)} fusion(bf16[768,4096]{1,0:T(8,128)(2,1)} %copy-done.2, bf16[768,256]{1,0:T(8,128)(2,1)} %bitcast.104), kind=kOutput, calls=%fused_computation.92 | convolution fusion | flops 1610612736 | bytes 10878976 | tf_op jit(solution)/shard_map/dot_general | solution.py:25
  142.6 2.1 all-to-all-done.5
  144.7 1.8 fusion.7
  146.6 4.8 %fusion.51 = f32[4096,256]{0,1:T(8,128)S(1)} fusion(bf16[768,4096]{1,0:T(8,128)(2,1)} %copy-done.3, bf16[768,256]{1,0:T(8,128)(2,1)S(1)} %bitcast.102), kind=kOutput, calls=%fused_computation.91 | convolution fusion | flops 1610612736 | bytes 10878976 | tf_op jit(solution)/shard_map/dot_general | solution.py:25
  151.4 3.8 %pad_maximum_fusion = f32[4096,512]{0,1:T(8,128)} fusion(f32[4096,256]{0,1:T(8,128)S(1)} %copy-done.1, f32[4096,256]{0,1:T(8,128)S(1)} %fusion.51), kind=kLoop, calls=%fused_computation.8 | loop fusion | flops 2097152 | bytes 16777216 | tf_op jit(solution)/shard_map/concatenate | solution.py:168
  155.2 0.9 copy-done.8
  156.3 0.4 fusion.21
  156.6 0.2 fusion.32
  156.8 3.5 %all-reduce.1 = (f32[16,2,256]{2,0,1:T(8,128)S(1)}, f32[2,256]{1,0:T(2,128)S(1)}) all-reduce(f32[16,2,256]{2,0,1:T(8,128)S(1)} %fusion.32, f32[2,256]{1,0:T(2,128)S(1)} %bitcast.116), channel_id=1, replica_groups=mesh['expert'=16,'dp'=2] {'dp'}, use_global_device_ids=true, to_apply=%region_9.10 | all-reduce | flops 8704 | bytes 69632 | tf_op jit(solution)/shard_map/psum | solution.py:180
  160.3 75.7 %all-reduce = (f32[16,2,256]{2,0,1:T(8,128)S(1)}, f32[2,256]{1,0:T(2,128)}) all-reduce(f32[16,2,256]{2,0,1:T(8,128)S(1)} %get-tuple-element.39, f32[2,256]{1,0:T(2,128)S(1)} %get-tuple-element.40), channel_id=1, replica_groups=mesh['expert'=16,'dp'=2] {'expert'}, use_global_device_ids=true, to_apply=%region_10.11 | all-reduce | flops 8704 | bytes 69632 | tf_op jit(solution)/shard_map/psum | solution.py:180
  236.0 0.6 copy.131
  236.6 2.6 %multiply_subtract_fusion = f32[1024,256]{1,0:T(8,128)} fusion(f32[1024,256]{1,0:T(8,128)} %param.23, f32[1024,256]{1,0:T(8,128)} %all-reduce.4.cloned.1.call-done), kind=kLoop, calls=%fused_computation.25 | loop fusion | flops 524288 | bytes 3145728 | tf_op jit(solution)/shard_map/sub | solution.py:189
  239.2 4.7 %slice_bitcast_fusion = (f32[1,2048,256]{1,2,0:T(8,128)}, f32[1,2048,256]{1,2,0:T(8,128)}) fusion(f32[2048,512]{0,1:T(8,128)} %reduce-scatter.2.cloned.1.call-done), kind=kLoop, calls=%fused_computation.9 | loop fusion | bytes 8388608 | tf_op jit(solution)/shard_map/broadcast_in_dim | solution.py:176
  243.9 2.9 %copy.129 = f32[1,2048,256]{2,1,0:T(8,128)} copy(f32[1,2048,256]{1,2,0:T(8,128)} %get-tuple-element.48) | data formatting | bytes 4194304
  246.8 2.9 %copy.130 = f32[1,2048,256]{2,1,0:T(8,128)} copy(f32[1,2048,256]{1,2,0:T(8,128)} %get-tuple-element.47) | data formatting | bytes 4194304
  (84 shorter events, 2.7 us)
Async XLA Ops:
  7.2 29.0 %copy-start = (bf16[1,4096,256]{2,1,0:T(8,128)(2,1)S(1)}, bf16[1,4096,256]{2,1,0:T(8,128)(2,1)}, u32[]{:S(2)}) copy-start(bf16[1,4096,256]{2,1,0:T(8,128)(2,1)} %param.15) | copy-start | bytes 6291460
  15.2 21.0 %all-to-all-start = ((bf16[16,48,256]{2,1,0:T(8,128)(2,1)}), bf16[16,48,256]{2,1,0:T(8,128)(2,1)S(1)}, u32[]{:S(2)}, u32[]{:S(2)}) async-start(bf16[16,48,256]{2,1,0:T(8,128)(2,1)} %bitcast.5), calls=%async_computation | async-start | bytes 786432 | tf_op jit(solution)/shard_map/all_to_all | solution.py:61
  36.1 6.5 %copy-start.4 = (bf16[16,48,256]{2,1,0:T(8,128)(2,1)}, bf16[16,48,256]{2,1,0:T(8,128)(2,1)S(1)}, u32[]{:S(2)}) copy-start(bf16[16,48,256]{2,1,0:T(8,128)(2,1)S(1)} %all-to-all-done) | copy-start | bytes 1179652
  36.1 9.1 %copy-start.23 = (bf16[1,4096,256]{2,1,0:T(8,128)(2,1)S(1)}, bf16[1,4096,256]{2,1,0:T(8,128)(2,1)}, u32[]{:S(2)}) copy-start(bf16[1,4096,256]{2,1,0:T(8,128)(2,1)} %param.16) | copy-start | bytes 6291460
  42.6 2.6 %copy-start.2 = (bf16[768,4096]{1,0:T(8,128)(2,1)}, bf16[768,4096]{1,0:T(8,128)(2,1)S(1)}, u32[]{:S(2)}) copy-start(bf16[768,4096]{1,0:T(8,128)(2,1)S(1)} %get-tuple-element.57) | copy-start | bytes 18874372
  45.2 8.1 %copy-start.19 = (s32[512]{0:T(512)S(1)}, s32[512]{0:T(512)}, u32[]{:S(2)}) copy-start(s32[512]{0:T(512)} %param.20) | copy-start | bytes 6148
  47.7 22.0 %copy-start.18 = (f32[2,256]{1,0:T(2,128)S(1)}, f32[2,256]{1,0:T(2,128)}, u32[]{:S(2)}) copy-start(f32[2,256]{1,0:T(2,128)} %param.18) | copy-start | bytes 6148
  47.7 23.3 %copy-start.21 = (s32[256,2]{0,1:T(2,128)S(1)}, s32[256,2]{0,1:T(2,128)}, u32[]{:S(2)}) copy-start(s32[256,2]{0,1:T(2,128)} %param.14) | copy-start | bytes 6148
  47.7 23.3 %copy-start.22 = (f32[2]{0:T(128)S(1)}, f32[2]{0:T(128)}, u32[]{:S(2)}) copy-start(f32[2]{0:T(128)} %param.19) | copy-start | bytes 28
  47.7 15.8 %all-to-all-start.1 = ((bf16[16,48,256]{2,1,0:T(8,128)(2,1)}), bf16[16,48,256]{2,1,0:T(8,128)(2,1)S(1)}, u32[]{:S(2)}, u32[]{:S(2)}) async-start(bf16[16,48,256]{2,1,0:T(8,128)(2,1)} %bitcast.9), calls=%async_computation.1 | async-start | bytes 786432 | tf_op jit(solution)/shard_map/all_to_all | solution.py:69
  53.0 14.2 %copy-start.13 = (f32[256,2,1]{0,1,2:T(2,128)}, f32[256,2,1]{0,1,2:T(2,128)S(1)}, u32[]{:S(2)}) copy-start(f32[256,2,1]{0,1,2:T(2,128)S(1)} %get-tuple-element.46) | copy-start | bytes 6148
  54.0 15.7 %copy-start.15 = (s32[1024]{0:T(1024)}, s32[1024]{0:T(1024)S(1)}, u32[]{:S(2)}) copy-start(s32[1024]{0:T(1024)S(1)} %pad_clamp_fusion.1) | copy-start | bytes 12292
  63.5 14.4 %all-to-all-start.3 = ((s32[16,1,32]{2,1,0:T(1,128)}), s32[16,1,32]{2,1,0:T(1,128)S(1)}, u32[]{:S(2)}, u32[]{:S(2)}) async-start(s32[16,1,32]{2,1,0:T(1,128)} %all_to_all.24), calls=%async_computation.4 | async-start | bytes 16384 | tf_op jit(solution)/shard_map/all_to_all | solution.py:158
  71.1 1.7 copy-start.11
  78.0 0.6 copy-start.10
  78.6 18.0 %all-to-all-start.2 = ((bf16[16,48,256]{2,1,0:T(8,128)(2,1)}), bf16[16,48,256]{2,1,0:T(8,128)(2,1)S(1)}, u32[]{:S(2)}, u32[]{:S(2)}) async-start(bf16[16,48,256]{2,1,0:T(8,128)(2,1)} %bitcast.14), calls=%async_computation.2 | async-start | bytes 786432 | tf_op jit(solution)/shard_map/all_to_all | solution.py:123
  96.5 8.8 %copy-start.6 = (bf16[16,48,256]{2,1,0:T(8,128)(2,1)}, bf16[16,48,256]{2,1,0:T(8,128)(2,1)S(1)}, u32[]{:S(2)}) copy-start(bf16[16,48,256]{2,1,0:T(8,128)(2,1)S(1)} %all-to-all-done.2) | copy-start | bytes 1179652
  105.3 2.7 %copy-start.3 = (bf16[768,4096]{1,0:T(8,128)(2,1)}, bf16[768,4096]{1,0:T(8,128)(2,1)S(1)}, u32[]{:S(2)}) copy-start(bf16[768,4096]{1,0:T(8,128)(2,1)S(1)} %multiply_convert_fusion) | copy-start | bytes 18874372
  108.0 7.9 %copy-start.14 = (f32[256,2,1]{0,1,2:T(2,128)S(1)}, f32[256,2,1]{0,1,2:T(2,128)}, u32[]{:S(2)}) copy-start(f32[256,2,1]{0,1,2:T(2,128)} %copy-done.13) | copy-start | bytes 6148
  108.0 17.8 %copy-start.16 = (s32[1024]{0:T(1024)S(1)}, s32[1024]{0:T(1024)}, u32[]{:S(2)}) copy-start(s32[1024]{0:T(1024)} %copy-done.15) | copy-start | bytes 12292
  110.5 17.9 %copy-start.9 = (bf16[16,2,256]{2,1,0:T(2,128)(2,1)S(1)}, bf16[16,2,256]{2,1,0:T(2,128)(2,1)}, u32[]{:S(2)}) copy-start(bf16[16,2,256]{2,1,0:T(2,128)(2,1)} %param.17) | copy-start | bytes 49156
  110.5 19.2 %copy-start.17 = (s32[1024]{0:T(1024)S(1)}, s32[1024]{0:T(1024)}, u32[]{:S(2)}) copy-start(s32[1024]{0:T(1024)} %pad_clamp_fusion) | copy-start | bytes 12292
  110.5 15.3 %all-to-all-start.4 = ((bf16[16,48,256]{2,1,0:T(8,128)(2,1)}), bf16[16,48,256]{2,1,0:T(8,128)(2,1)S(1)}, u32[]{:S(2)}, u32[]{:S(2)}) async-start(bf16[16,48,256]{2,1,0:T(8,128)(2,1)} %bitcast.107), calls=%async_computation.5 | async-start | bytes 786432 | tf_op jit(solution)/shard_map/all_to_all | solution.py:139
  132.1 12.5 %all-to-all-start.5 = ((bf16[16,32,256]{2,1,0:T(8,128)(2,1)}), bf16[16,32,256]{2,1,0:T(8,128)(2,1)S(1)}, u32[]{:S(2)}, u32[]{:S(2)}) async-start(bf16[16,32,256]{2,1,0:T(8,128)(2,1)} %multiply_convert_fusion.2), calls=%async_computation.6 | async-start | bytes 524288 | tf_op jit(solution)/shard_map/all_to_all | solution.py:157
  135.8 8.9 %copy-start.20 = (s32[512]{0:T(512)S(1)}, s32[512]{0:T(512)}, u32[]{:S(2)}) copy-start(s32[512]{0:T(512)} %eq.64) | copy-start | bytes 6148
  135.8 10.7 %copy-start.5 = (bf16[16,48,256]{2,1,0:T(8,128)(2,1)S(1)}, bf16[16,48,256]{2,1,0:T(8,128)(2,1)}, u32[]{:S(2)}) copy-start(bf16[16,48,256]{2,1,0:T(8,128)(2,1)} %copy-done.4) | copy-start | bytes 1179652
  135.8 100.8 %all-reduce.4.cloned.1.call-start = ((), (), s32[]{:S(2)}) async-start(), calls=%async_computation.8 | async-start | bytes 2097152 | tf_op jit(solution)/shard_map/psum | solution.py:188
  146.5 92.7 %reduce-scatter.2.cloned.1.call-start = ((), (), s32[]{:S(2)}) async-start(), calls=%async_computation.7 | async-start | bytes 12582912 | tf_op jit(solution)/shard_map/reduce_scatter | solution.py:167
  146.5 4.8 %copy-start.1 = (f32[4096,256]{0,1:T(8,128)S(1)}, f32[4096,256]{0,1:T(8,128)}, u32[]{:S(2)}) copy-start(f32[4096,256]{0,1:T(8,128)} %fusion.52) | copy-start | bytes 12582916
  155.1 0.9 copy-start.8
  155.1 1.1 copy-start.12
  155.1 1.5 copy-start.7
Sparse Core Ops, SparseCore 0:
  146.6 18.6 all-reduce.3
  167.6 17.4 reduce-scatter.1
